TPU v7x, 768 devices: a whole 4x8x12 slice. The times are simulated.
768 devices in a mesh: view: 48 (over z_lo, y, core), tok: 16 (over x, z_hi).
Axes of the slice: x: 4, y: 8, z: 12 (z_hi: 4, z_lo: 3; z = z_hi * 3 + z_lo), core: 2. Of those that a mesh axis runs over, the one named last changes fastest.
Arguments:
- queries: bfloat16 [48, 2048, 2048], P('view', 'tok'), may hold values from -6 to 6
- key_states: bfloat16 [48, 2048, 2048], P('view', 'tok'), may hold values from -6 to 6
- value_states: bfloat16 [48, 2048, 2048], P('view', 'tok'), may hold values from -6 to 6
- grad_output: bfloat16 [48, 2048, 2048], P('view', 'tok'), may hold values from -6 to 6
- counts: int32 [48, 16], replicated, may hold values from 8 to 128, as said below
- matching: int32 [1, 48], P(None, 'view'), may hold values from 0 to 47, as said below
Outputs:
- attended: bfloat16 [48, 2048, 2048], P('view', 'tok')
- grad_queries: bfloat16 [48, 2048, 2048], P('view', 'tok')
- grad_keys: bfloat16 [48, 2048, 2048], P('view', 'tok')
- grad_values: bfloat16 [48, 2048, 2048], P('view', 'tok')
Inputs may be any that keep to these rules, and one draw needn't show every extreme that they name: The valid tokens of shard t of view v are its first counts[v, t] positions; every view holds exactly 640 valid tokens, and in every view some shard has all 128 positions valid. In every round each view is paired with one of its two neighbours on the cycle of 48 views, the one before or the one after, and pairs are mutual: matching[r, matching[r, v]] = v.
All inputs are finite; a program needn't handle non-finite values.
Results may differ from a plain program's by a relative error of at most 0.0092.
Values may be sent and summed in bfloat16 or wider, within the bound.
No kernel may reach another device: no remote copies, remote signals or barrier semaphores. Data moves between devices by JAX's collectives and lax.ppermute only.
A program may use at most 32 MiB of HBM per device.

v0:
```python
import functools
import math

import jax
import jax.numpy as jnp
from jax import lax
from jax.experimental import pallas as pl
from jax.experimental.pallas import tpu as pltpu
from jax.sharding import PartitionSpec as P

NEG_FILL = -1e30
KERNEL_BYTES = 20 << 20
WIDE = jnp.float32
LOW = jnp.bfloat16


def matmul(left, right, left_dim, right_dim):
    return lax.dot_general(
        left, right, (((left_dim,), (right_dim,)), ((), ())), preferred_element_type=WIDE
    )


def softmax_rows(scores):
    exponent = jnp.exp(scores - jnp.max(scores, axis=-1, keepdims=True))
    return exponent * (1.0 / jnp.sum(exponent, axis=-1, keepdims=True))


def score_gradient(weights, value_gradient, logit_scale):
    row_delta = jnp.sum(weights * value_gradient, axis=-1, keepdims=True)
    return (weights * (value_gradient - row_delta) * logit_scale).astype(LOW)


def split_heads(arrays, group):
    rows, width = arrays[0].shape
    heads = width // 128

    def body(*refs):
        out_ref = refs[-1]
        for j, ref in enumerate(refs[:-1]):
            for h in range(group):
                out_ref[h, j] = ref[:, h * 128 : (h + 1) * 128]

    return pl.pallas_call(
        body,
        grid=(heads // group,),
        in_specs=[pl.BlockSpec((rows, group * 128), lambda i: (0, i))] * len(arrays),
        out_specs=pl.BlockSpec((group, len(arrays), rows, 128), lambda i: (i, 0, 0, 0)),
        out_shape=jax.ShapeDtypeStruct((heads, len(arrays), rows, 128), LOW),
        name="split_heads",
    )(*arrays)


def global_body(counts_ref, x_ref, y_ref, wide_ref, low_ref, back_ref, *, total, logit_scale):
    shards, parts, rows, head_dim = x_ref.shape
    starts = []
    start = 0
    for t in range(shards):
        starts.append(start)
        start = start + counts_ref[t]
    for t in range(shards):
        for j in range(parts):
            wide_ref[j, pl.ds(starts[t], rows), :] = x_ref[t, j].astype(WIDE)
    for j in range(parts):
        low_ref[j] = wide_ref[j, :total].astype(LOW)
    key = low_ref[1]
    value = low_ref[2]
    step = 128
    for at in range(0, total, step):
        query = low_ref[0, at : at + step]
        grad = low_ref[3, at : at + step]
        weights = softmax_rows(matmul(query, key, 1, 1) * logit_scale)
        weights_low = weights.astype(LOW)
        wide_ref[0, at : at + step] = matmul(weights_low, value, 1, 0)
        value_part = matmul(grad, weights_low, 0, 0)
        score_low = score_gradient(weights, matmul(grad, value, 1, 1), logit_scale)
        wide_ref[1, at : at + step] = matmul(score_low, key, 1, 0)
        key_part = matmul(query, score_low, 0, 0)
        if at == 0:
            back_ref[0] = key_part
            back_ref[1] = value_part
        else:
            back_ref[0] += key_part
            back_ref[1] += value_part
    wide_ref[2, :total] = back_ref[0].T
    wide_ref[3, :total] = back_ref[1].T
    for t in range(shards):
        for j in range(parts):
            y_ref[t, j] = wide_ref[j, pl.ds(starts[t], rows), :].astype(LOW)


def global_attention(own_counts, stacked, total, logit_scale):
    shards, parts, rows, head_dim = stacked.shape
    return pl.pallas_call(
        functools.partial(global_body, total=total, logit_scale=logit_scale),
        in_specs=[
            pl.BlockSpec(memory_space=pltpu.SMEM),
            pl.BlockSpec(memory_space=pltpu.VMEM),
        ],
        out_specs=pl.BlockSpec(memory_space=pltpu.VMEM),
        out_shape=jax.ShapeDtypeStruct(stacked.shape, LOW),
        scratch_shapes=[
            pltpu.VMEM((parts, total + rows, head_dim), WIDE),
            pltpu.VMEM((parts, total, head_dim), LOW),
            pltpu.VMEM((2, head_dim, total), WIDE),
        ],
        compiler_params=pltpu.CompilerParams(vmem_limit_bytes=KERNEL_BYTES),
        name="global_attention",
    )(own_counts, stacked)


def band_body(pair_ref, own_ref, other_ref, out_ref, *, logit_scale):
    group, parts, rows, head_dim = own_ref.shape
    own_count = pair_ref[0]
    other_count = pair_ref[1]
    columns = lax.broadcasted_iota(jnp.int32, (rows, rows), 1)
    row_ids = lax.broadcasted_iota(jnp.int32, (rows, head_dim), 0)
    zero_low = jnp.zeros((), LOW)
    for h in range(group):
        query, key, value, grad = (own_ref[h, j] for j in range(4))
        other_query, other_key, other_value, other_grad = (other_ref[h, j] for j in range(4))
        grad = jnp.where(row_ids < own_count, grad, zero_low)
        other_grad = jnp.where(row_ids < other_count, other_grad, zero_low)
        scores = matmul(query, other_key, 1, 1) * logit_scale
        weights = softmax_rows(jnp.where(columns < other_count, scores, NEG_FILL))
        out_ref[h, 0] = matmul(weights.astype(LOW), other_value, 1, 0).astype(LOW)
        score_low = score_gradient(weights, matmul(grad, other_value, 1, 1), logit_scale)
        out_ref[h, 1] = matmul(score_low, other_key, 1, 0).astype(LOW)
        scores = matmul(other_query, key, 1, 1) * logit_scale
        weights = softmax_rows(jnp.where(columns < own_count, scores, NEG_FILL))
        out_ref[h, 3] = matmul(weights.astype(LOW), other_grad, 0, 0).astype(LOW)
        score_low = score_gradient(weights, matmul(other_grad, value, 1, 1), logit_scale)
        out_ref[h, 2] = matmul(score_low, other_query, 0, 0).astype(LOW)


def band_attention(pair_counts, own, other, group, logit_scale):
    heads, parts, rows, head_dim = own.shape
    block = pl.BlockSpec((group, parts, rows, head_dim), lambda i: (i, 0, 0, 0))
    return pl.pallas_call(
        functools.partial(band_body, logit_scale=logit_scale),
        grid=(heads // group,),
        in_specs=[pl.BlockSpec(memory_space=pltpu.SMEM), block, block],
        out_specs=block,
        out_shape=jax.ShapeDtypeStruct(own.shape, LOW),
        compiler_params=pltpu.CompilerParams(vmem_limit_bytes=KERNEL_BYTES),
        name="band_attention",
    )(pair_counts, own, other)


def merge_body(pair_ref, back_ref, band_ref, *out_refs):
    group, parts, rows, head_dim = back_ref.shape
    keep = lax.broadcasted_iota(jnp.int32, (rows, head_dim), 0) < pair_ref[0]
    for j in range(parts):
        for h in range(group):
            total = back_ref[h, j].astype(WIDE) + band_ref[h, j].astype(WIDE)
            out_refs[j][:, h * head_dim : (h + 1) * head_dim] = jnp.where(keep, total, 0.0).astype(
                LOW
            )


def merge(pair_counts, back, band, group):
    heads, parts, rows, head_dim = back.shape
    block = pl.BlockSpec((group, parts, rows, head_dim), lambda i: (i, 0, 0, 0))
    flat = pl.BlockSpec((rows, group * head_dim), lambda i: (0, i))
    return pl.pallas_call(
        merge_body,
        grid=(heads // group,),
        in_specs=[pl.BlockSpec(memory_space=pltpu.SMEM), block, block],
        out_specs=[flat] * parts,
        out_shape=[jax.ShapeDtypeStruct((rows, heads * head_dim), LOW)] * parts,
        compiler_params=pltpu.CompilerParams(vmem_limit_bytes=KERNEL_BYTES),
        name="merge",
    )(pair_counts, back, band)


def exchange(array, on_right, view_index, view_count):
    def swap(parity):
        pairs = [
            (v, (v + 1) % view_count if (v - parity) % 2 == 0 else (v - 1) % view_count)
            for v in range(view_count)
        ]
        return lambda a: lax.ppermute(a, "view", pairs)

    even_first = on_right == (view_index % 2 == 0)
    return lax.cond(even_first, swap(0), swap(1), array)


def to_heads(array):
    return lax.all_to_all(array, "tok", split_axis=0, concat_axis=0, tiled=True)


def view_body(queries, key_states, value_states, grad_output, counts, matching):
    view_index = lax.axis_index("view")
    shard_index = lax.axis_index("tok")
    view_count = lax.axis_size("view")
    shard_count = lax.axis_size("tok")
    shard_rows, row_width = queries.shape
    head_dim = row_width // shard_count
    packed_rows = 5 * shard_rows * shard_count // 16
    logit_scale = 1.0 / math.sqrt(head_dim)
    partner = matching[0, 0]
    on_right = partner == (view_index + 1) % view_count
    own_counts = lax.dynamic_index_in_dim(counts, view_index, 0, keepdims=False)
    pair_counts = jnp.stack([counts[view_index, shard_index], counts[partner, shard_index]])
    stacked = split_heads((queries, key_states, value_states, grad_output), 4)
    gathered = to_heads(stacked)
    other = exchange(stacked, on_right, view_index, view_count)
    band = band_attention(pair_counts, stacked, other, 2, logit_scale)
    gathered, band = lax.optimization_barrier((gathered, band))
    back = to_heads(global_attention(own_counts, gathered, packed_rows, logit_scale))
    return merge(pair_counts, back, band, 4)


def per_device(queries, key_states, value_states, grad_output, counts, matching):
    results = view_body(
        queries[0], key_states[0], value_states[0], grad_output[0], counts, matching
    )
    return tuple((result[None] for result in results))


def solution(mesh):
    split = P("view", "tok", None)
    return jax.shard_map(
        per_device,
        mesh=mesh,
        in_specs=(split, split, split, split, P(), P(None, "view")),
        out_specs=(split, split, split, split),
        check_vma=False,
    )
```

profile of v0, /device:TPU:97, one launch (start us, length us, event | category | flops | bytes accessed | tf_op | source)
XLA Modules:
  0.0 186.9 jit_solution(10063886922041652703)
XLA Ops:
  0.6 4.0 %split_heads.1.own_ref = bf16[16,4,128,128]{3,2,1,0:T(8,128)(2,1)} custom-call(bf16[128,2048]{1,0:T(8,128)(2,1)} %bitcast.15, bf16[128,2048]{1,0:T(8,128)(2,1)} %bitcast.16, bf16[128,2048]{1,0:T(8,128)(2,1)} %bitcast.17, bf16[128,2048]{1,0:T(8,128)(2,1)} %bitcast.18), custom_call_target="tpu_custom_call" | custom-call | tf_op jit(solution)/shard_map/split_heads/pallas_call | solution.py:43
  4.6 0.0 copy-start
  4.6 16.1 %all-to-all-start = ((bf16[16,4,128,128]{3,2,1,0:T(8,128)(2,1)}), bf16[16,4,128,128]{3,2,1,0:T(8,128)(2,1)}, u32[]{:S(2)}, u32[]{:S(2)}) async-start(bf16[16,4,128,128]{3,2,1,0:T(8,128)(2,1)} %split_heads.1.own_ref), calls=%async_computation | async-start | bytes 4194304 | tf_op jit(solution)/shard_map/all_to_all | solution.py:188
  21.3 7.0 %conditional.1 = (bf16[16,4,128,128]{3,2,1,0:T(8,128)(2,1)}) conditional(s32[]{:T(128)} %convert_element_type.3, bf16[16,4,128,128]{3,2,1,0:T(8,128)(2,1)} %split_heads.1.own_ref, bf16[16,4,128,128]{3,2,1,0:T(8,128)(2,1)} %split_heads.1.own_ref), branch_computations={%region_0.1_spmd, %region_1.2_spmd} | conditional | bytes 8388656 | solution.py:184
  21.4 2.9 %collective-permute-start.1 = (bf16[16,4,128,128]{3,2,1,0:T(8,128)(2,1)}, bf16[16,4,128,128]{3,2,1,0:T(8,128)(2,1)}, u32[]{:S(2)}, u32[]{:S(2)}) collective-permute-start(bf16[16,4,128,128]{3,2,1,0:T(8,128)(2,1)} %param.1), channel_id=1, source_target_pairs={{0,16},{16,0},{32,48},{48,32},{64,80},{80,64},{96,112},{112,96},{1... | collective-permute-start | bytes 6291464 | tf_op jit(solution)/shard_map/cond/branch_1_fun/ppermute | solution.py:181
  24.2 4.1 %collective-permute-done.1 = bf16[16,4,128,128]{3,2,1,0:T(8,128)(2,1)} collective-permute-done((bf16[16,4,128,128]{3,2,1,0:T(8,128)(2,1)}, bf16[16,4,128,128]{3,2,1,0:T(8,128)(2,1)}, u32[]{:S(2)}, u32[]{:S(2)}) %collective-permute-start.1) | collective-permute-done | bytes 2097184 | tf_op jit(solution)/shard_map/cond/branch_1_fun/ppermute | solution.py:181
  28.3 0.0 copy-done
  28.3 0.6 fusion
  28.9 1.4 pad_add_fusion.pair_ref
  30.3 21.9 %band_attention.1.band_ref = bf16[16,4,128,128]{3,2,1,0:T(8,128)(2,1)S(1)} custom-call(s32[2]{0:T(128)S(1)} %pad_add_fusion.pair_ref, bf16[16,4,128,128]{3,2,1,0:T(8,128)(2,1)} %split_heads.1.own_ref, bf16[16,4,128,128]{3,2,1,0:T(8,128)(2,1)} %get-tuple-element.23.other_ref), custom_call_target="tpu_custom_call" | custom-call | tf_op jit(solution)/shard_map/band_attention/pallas_call | solution.py:138
  52.2 0.2 dynamic-slice_reduce_fusion.counts_ref
  52.4 45.5 %all-to-all-done.x_ref = bf16[16,4,128,128]{3,2,1,0:T(8,128)(2,1)} async-done(((bf16[16,4,128,128]{3,2,1,0:T(8,128)(2,1)}), bf16[16,4,128,128]{3,2,1,0:T(8,128)(2,1)}, u32[]{:S(2)}, u32[]{:S(2)}) %all-to-all-start) | async-done | bytes 2097184 | tf_op jit(solution)/shard_map/all_to_all | solution.py:188
  97.9 6.4 %global_attention.1 = bf16[16,4,128,128]{3,2,1,0:T(8,128)(2,1)S(1)} custom-call(s32[16]{0:T(128)S(1)} %dynamic-slice_reduce_fusion.counts_ref, bf16[16,4,128,128]{3,2,1,0:T(8,128)(2,1)} %all-to-all-done.x_ref), custom_call_target="tpu_custom_call" | custom-call | tf_op jit(solution)/shard_map/global_attention/pallas_call | solution.py:93
  104.3 80.1 %all_to_all.10.back_ref = bf16[16,4,128,128]{3,2,1,0:T(8,128)(2,1)S(1)} all-to-all(bf16[16,4,128,128]{3,2,1,0:T(8,128)(2,1)S(1)} %global_attention.1), channel_id=1, replica_groups=mesh['view'=48,'tok'=16] {'tok'}, dimensions={0} | all-to-all | bytes 4194304 | tf_op jit(solution)/shard_map/all_to_all | solution.py:188
  184.4 2.4 %merge.1 = (bf16[128,2048]{1,0:T(8,128)(2,1)}, bf16[128,2048]{1,0:T(8,128)(2,1)}, bf16[128,2048]{1,0:T(8,128)(2,1)}, bf16[128,2048]{1,0:T(8,128)(2,1)}) custom-call(s32[2]{0:T(128)S(1)} %pad_add_fusion.pair_ref, bf16[16,4,128,128]{3,2,1,0:T(8,128)(2,1)S(1)} %all_to_all.10.back_ref, bf16[16,4,128,128]{3,2,1,0:T(8,128)(2,1)S(1)} %band_attention.1.band_ref), custom_call_target="tpu_custom_call" | custom-call | tf_op jit(solution)/shard_map/merge/pallas_call | solution.py:164
Async XLA Ops:
  4.6 23.8 %copy-start = (s32[48,16]{0,1:T(8,128)S(1)}, s32[48,16]{0,1:T(8,128)}, u32[]{:S(2)}) copy-start(s32[48,16]{0,1:T(8,128)} %param.12) | copy-start | bytes 9220
  4.6 93.3 %all-to-all-start = ((bf16[16,4,128,128]{3,2,1,0:T(8,128)(2,1)}), bf16[16,4,128,128]{3,2,1,0:T(8,128)(2,1)}, u32[]{:S(2)}, u32[]{:S(2)}) async-start(bf16[16,4,128,128]{3,2,1,0:T(8,128)(2,1)} %split_heads.1.own_ref), calls=%async_computation | async-start | bytes 4194304 | tf_op jit(solution)/shard_map/all_to_all | solution.py:188
  21.4 7.0 %collective-permute-start.1 = (bf16[16,4,128,128]{3,2,1,0:T(8,128)(2,1)}, bf16[16,4,128,128]{3,2,1,0:T(8,128)(2,1)}, u32[]{:S(2)}, u32[]{:S(2)}) collective-permute-start(bf16[16,4,128,128]{3,2,1,0:T(8,128)(2,1)} %param.1), channel_id=1, source_target_pairs={{0,16},{16,0},{32,48},{48,32},{64,80},{80,64},{96,112},{112,96},{1... | collective-permute-start | bytes 6291464 | tf_op jit(solution)/shard_map/cond/branch_1_fun/ppermute | solution.py:181
where the time goes:
time: 187 us
  blocking collectives  80.1 us (43%)
  waiting for transfers between devices  49.6 us (27%)
  Pallas kernels  34.7 us (19%)
  starting transfers between devices  18.9 us (10%)
    all_to_all x1, blocking collectives, to_heads(): return lax.all_to_all(array, 'tok', split_axis=0, concat_axis=0, tiled=True)  80.1 us
    all_to_all x1, waiting for transfers between devices, to_heads(): return lax.all_to_all(array, 'tok', split_axis=0, concat_axis=0, tiled=True)  45.5 us
    pallas_call x1, Pallas kernels, band_attention(): pl.pallas_call(functools.partial(band_body, logit_scale=logit_scale), gri...  21.9 us
    all_to_all x1, starting transfers between devices, to_heads(): return lax.all_to_all(array, 'tok', split_axis=0, concat_axis=0, tiled=True)  16.1 us
    pallas_call x1, Pallas kernels, global_attention(): pl.pallas_call(functools.partial(global_body, total=total, logit_scale=lo...  6.37 us
    ppermute x1, waiting for transfers between devices, swap(): return lambda a: lax.ppermute(a, 'view', pairs)  4.11 us
    pallas_call x1, Pallas kernels, split_heads(): pl.pallas_call(body, grid=(heads // group,), in_specs=[pl.BlockSpec((rows...  3.95 us
  transfers between devices with their start and end apart: 2, of which 2 were waited for; matrix products, arithmetic and copies ran while one was open for 1% of the time, Pallas kernels for 12%

commit v1 on v0

--- a/solution.py
+++ b/solution.py
@@ -10,6 +10,7 @@
 
 NEG_FILL = -1e30
 KERNEL_BYTES = 20 << 20
+BAND_HEADS = 4
 WIDE = jnp.float32
 LOW = jnp.bfloat16
 
@@ -115,21 +116,28 @@
     columns = lax.broadcasted_iota(jnp.int32, (rows, rows), 1)
     row_ids = lax.broadcasted_iota(jnp.int32, (rows, head_dim), 0)
     zero_low = jnp.zeros((), LOW)
+    own = [[own_ref[h, j] for j in range(4)] for h in range(group)]
+    other = [[other_ref[h, j] for j in range(4)] for h in range(group)]
     for h in range(group):
-        query, key, value, grad = (own_ref[h, j] for j in range(4))
-        other_query, other_key, other_value, other_grad = (other_ref[h, j] for j in range(4))
-        grad = jnp.where(row_ids < own_count, grad, zero_low)
-        other_grad = jnp.where(row_ids < other_count, other_grad, zero_low)
-        scores = matmul(query, other_key, 1, 1) * logit_scale
-        weights = softmax_rows(jnp.where(columns < other_count, scores, NEG_FILL))
-        out_ref[h, 0] = matmul(weights.astype(LOW), other_value, 1, 0).astype(LOW)
-        score_low = score_gradient(weights, matmul(grad, other_value, 1, 1), logit_scale)
-        out_ref[h, 1] = matmul(score_low, other_key, 1, 0).astype(LOW)
-        scores = matmul(other_query, key, 1, 1) * logit_scale
-        weights = softmax_rows(jnp.where(columns < own_count, scores, NEG_FILL))
-        out_ref[h, 3] = matmul(weights.astype(LOW), other_grad, 0, 0).astype(LOW)
-        score_low = score_gradient(weights, matmul(other_grad, value, 1, 1), logit_scale)
-        out_ref[h, 2] = matmul(score_low, other_query, 0, 0).astype(LOW)
+        own[h][3] = jnp.where(row_ids < own_count, own[h][3], zero_low)
+        other[h][3] = jnp.where(row_ids < other_count, other[h][3], zero_low)
+    sides = [(own[h], other[h], other_count) for h in range(group)]
+    sides += [(other[h], own[h], own_count) for h in range(group)]
+    scores = [matmul(a[0], b[1], 1, 1) for a, b, count in sides]
+    gradients = [matmul(a[3], b[2], 1, 1) for a, b, count in sides]
+    weights = [
+        softmax_rows(jnp.where(columns < side[2], part * logit_scale, NEG_FILL))
+        for part, side in zip(scores, sides)
+    ]
+    weights_low = [part.astype(LOW) for part in weights]
+    score_low = [
+        score_gradient(part, gradient, logit_scale) for part, gradient in zip(weights, gradients)
+    ]
+    for h in range(group):
+        out_ref[h, 0] = matmul(weights_low[h], other[h][2], 1, 0).astype(LOW)
+        out_ref[h, 1] = matmul(score_low[h], other[h][1], 1, 0).astype(LOW)
+        out_ref[h, 2] = matmul(score_low[group + h], other[h][0], 0, 0).astype(LOW)
+        out_ref[h, 3] = matmul(weights_low[group + h], other[h][3], 0, 0).astype(LOW)
 
 
 def band_attention(pair_counts, own, other, group, logit_scale):
@@ -204,9 +212,10 @@
     stacked = split_heads((queries, key_states, value_states, grad_output), 4)
     gathered = to_heads(stacked)
     other = exchange(stacked, on_right, view_index, view_count)
-    band = band_attention(pair_counts, stacked, other, 2, logit_scale)
+    band = band_attention(pair_counts, stacked, other, BAND_HEADS, logit_scale)
     gathered, band = lax.optimization_barrier((gathered, band))
-    back = to_heads(global_attention(own_counts, gathered, packed_rows, logit_scale))
+    parts = global_attention(own_counts, gathered, packed_rows, logit_scale)
+    back = to_heads(parts)
     return merge(pair_counts, back, band, 4)
 
 

time: 187 us -> 187 us (level)
  Pallas kernels: 34.7 us -> 18.2 us
  waiting for transfers between devices: 49.6 us -> 66 us
    pallas_call x1, Pallas kernels: 21.9 us -> 5.49 us  [band_attention(): pl.pallas_call(functools.partial(band_body, logit_scale=logit_scale), gri...]
    all_to_all x1, waiting for transfers between devices: 45.5 us -> 61.9 us  [to_heads(): return lax.all_to_all(array, 'tok', split_axis=0, concat_axis=0, tiled=True)]
  transfers between devices with their start and end apart: 2 -> 2, of which waited for: 2 -> 2; matrix products, arithmetic and copies ran while one was open for 1% -> 1% of each run, Pallas kernels for 12% -> 3%
where the time goes in v1:
time: 187 us
  blocking collectives  80.1 us (43%)
  waiting for transfers between devices  66 us (35%)
  starting transfers between devices  18.9 us (10%)
  Pallas kernels  18.2 us (10%)
    all_to_all x1, blocking collectives, to_heads(): return lax.all_to_all(array, 'tok', split_axis=0, concat_axis=0, tiled=True)  80.1 us
    all_to_all x1, waiting for transfers between devices, to_heads(): return lax.all_to_all(array, 'tok', split_axis=0, concat_axis=0, tiled=True)  61.9 us
    all_to_all x1, starting transfers between devices, to_heads(): return lax.all_to_all(array, 'tok', split_axis=0, concat_axis=0, tiled=True)  16.1 us
    pallas_call x1, Pallas kernels, global_attention(): pl.pallas_call(functools.partial(global_body, total=total, logit_scale=lo...  6.37 us
    pallas_call x1, Pallas kernels, band_attention(): pl.pallas_call(functools.partial(band_body, logit_scale=logit_scale), gri...  5.49 us
    ppermute x1, waiting for transfers between devices, swap(): return lambda a: lax.ppermute(a, 'view', pairs)  4.11 us
    pallas_call x1, Pallas kernels, split_heads(): pl.pallas_call(body, grid=(heads // group,), in_specs=[pl.BlockSpec((rows...  3.95 us
  transfers between devices with their start and end apart: 2, of which 2 were waited for; matrix products, arithmetic and copies ran while one was open for 1% of the time, Pallas kernels for 3%

profile of v1, /device:TPU:97, one launch (start us, length us, event | category | flops | bytes accessed | tf_op | source)
XLA Modules:
  0.0 186.9 jit_solution(14874860942757988633)
XLA Ops:
  0.6 4.0 %split_heads.1.own_ref = bf16[16,4,128,128]{3,2,1,0:T(8,128)(2,1)} custom-call(bf16[128,2048]{1,0:T(8,128)(2,1)} %bitcast.15, bf16[128,2048]{1,0:T(8,128)(2,1)} %bitcast.16, bf16[128,2048]{1,0:T(8,128)(2,1)} %bitcast.17, bf16[128,2048]{1,0:T(8,128)(2,1)} %bitcast.18), custom_call_target="tpu_custom_call" | custom-call | tf_op jit(solution)/shard_map/split_heads/pallas_call | solution.py:44
  4.6 0.0 copy-start
  4.6 16.1 %all-to-all-start = ((bf16[16,4,128,128]{3,2,1,0:T(8,128)(2,1)}), bf16[16,4,128,128]{3,2,1,0:T(8,128)(2,1)}, u32[]{:S(2)}, u32[]{:S(2)}) async-start(bf16[16,4,128,128]{3,2,1,0:T(8,128)(2,1)} %split_heads.1.own_ref), calls=%async_computation | async-start | bytes 4194304 | tf_op jit(solution)/shard_map/all_to_all | solution.py:196
  21.3 7.0 %conditional.1 = (bf16[16,4,128,128]{3,2,1,0:T(8,128)(2,1)}) conditional(s32[]{:T(128)} %convert_element_type.3, bf16[16,4,128,128]{3,2,1,0:T(8,128)(2,1)} %split_heads.1.own_ref, bf16[16,4,128,128]{3,2,1,0:T(8,128)(2,1)} %split_heads.1.own_ref), branch_computations={%region_0.1_spmd, %region_1.2_spmd} | conditional | bytes 8388656 | solution.py:192
  21.4 2.9 %collective-permute-start.1 = (bf16[16,4,128,128]{3,2,1,0:T(8,128)(2,1)}, bf16[16,4,128,128]{3,2,1,0:T(8,128)(2,1)}, u32[]{:S(2)}, u32[]{:S(2)}) collective-permute-start(bf16[16,4,128,128]{3,2,1,0:T(8,128)(2,1)} %param.1), channel_id=1, source_target_pairs={{0,16},{16,0},{32,48},{48,32},{64,80},{80,64},{96,112},{112,96},{1... | collective-permute-start | bytes 6291464 | tf_op jit(solution)/shard_map/cond/branch_1_fun/ppermute | solution.py:189
  24.2 4.1 %collective-permute-done.1 = bf16[16,4,128,128]{3,2,1,0:T(8,128)(2,1)} collective-permute-done((bf16[16,4,128,128]{3,2,1,0:T(8,128)(2,1)}, bf16[16,4,128,128]{3,2,1,0:T(8,128)(2,1)}, u32[]{:S(2)}, u32[]{:S(2)}) %collective-permute-start.1) | collective-permute-done | bytes 2097184 | tf_op jit(solution)/shard_map/cond/branch_1_fun/ppermute | solution.py:189
  28.3 0.0 copy-done
  28.3 0.6 fusion
  28.9 1.4 pad_add_fusion.pair_ref
  30.3 5.5 %band_attention.1.band_ref = bf16[16,4,128,128]{3,2,1,0:T(8,128)(2,1)S(1)} custom-call(s32[2]{0:T(128)S(1)} %pad_add_fusion.pair_ref, bf16[16,4,128,128]{3,2,1,0:T(8,128)(2,1)} %split_heads.1.own_ref, bf16[16,4,128,128]{3,2,1,0:T(8,128)(2,1)} %get-tuple-element.23.other_ref), custom_call_target="tpu_custom_call" | custom-call | tf_op jit(solution)/shard_map/band_attention/pallas_call | solution.py:146
  35.8 0.2 dynamic-slice_reduce_fusion.counts_ref
  36.0 61.9 %all-to-all-done.x_ref = bf16[16,4,128,128]{3,2,1,0:T(8,128)(2,1)} async-done(((bf16[16,4,128,128]{3,2,1,0:T(8,128)(2,1)}), bf16[16,4,128,128]{3,2,1,0:T(8,128)(2,1)}, u32[]{:S(2)}, u32[]{:S(2)}) %all-to-all-start) | async-done | bytes 2097184 | tf_op jit(solution)/shard_map/all_to_all | solution.py:196
  97.9 6.4 %global_attention.1 = bf16[16,4,128,128]{3,2,1,0:T(8,128)(2,1)S(1)} custom-call(s32[16]{0:T(128)S(1)} %dynamic-slice_reduce_fusion.counts_ref, bf16[16,4,128,128]{3,2,1,0:T(8,128)(2,1)} %all-to-all-done.x_ref), custom_call_target="tpu_custom_call" | custom-call | tf_op jit(solution)/shard_map/global_attention/pallas_call | solution.py:94
  104.3 80.1 %all_to_all.10.back_ref = bf16[16,4,128,128]{3,2,1,0:T(8,128)(2,1)S(1)} all-to-all(bf16[16,4,128,128]{3,2,1,0:T(8,128)(2,1)S(1)} %global_attention.1), channel_id=1, replica_groups=mesh['view'=48,'tok'=16] {'tok'}, dimensions={0} | all-to-all | bytes 4194304 | tf_op jit(solution)/shard_map/all_to_all | solution.py:196
  184.5 2.4 %merge.1 = (bf16[128,2048]{1,0:T(8,128)(2,1)}, bf16[128,2048]{1,0:T(8,128)(2,1)}, bf16[128,2048]{1,0:T(8,128)(2,1)}, bf16[128,2048]{1,0:T(8,128)(2,1)}) custom-call(s32[2]{0:T(128)S(1)} %pad_add_fusion.pair_ref, bf16[16,4,128,128]{3,2,1,0:T(8,128)(2,1)S(1)} %all_to_all.10.back_ref, bf16[16,4,128,128]{3,2,1,0:T(8,128)(2,1)S(1)} %band_attention.1.band_ref), custom_call_target="tpu_custom_call" | custom-call | tf_op jit(solution)/shard_map/merge/pallas_call | solution.py:172
Async XLA Ops:
  4.6 23.8 %copy-start = (s32[48,16]{0,1:T(8,128)S(1)}, s32[48,16]{0,1:T(8,128)}, u32[]{:S(2)}) copy-start(s32[48,16]{0,1:T(8,128)} %param.12) | copy-start | bytes 9220
  4.6 93.3 %all-to-all-start = ((bf16[16,4,128,128]{3,2,1,0:T(8,128)(2,1)}), bf16[16,4,128,128]{3,2,1,0:T(8,128)(2,1)}, u32[]{:S(2)}, u32[]{:S(2)}) async-start(bf16[16,4,128,128]{3,2,1,0:T(8,128)(2,1)} %split_heads.1.own_ref), calls=%async_computation | async-start | bytes 4194304 | tf_op jit(solution)/shard_map/all_to_all | solution.py:196
  21.4 7.0 %collective-permute-start.1 = (bf16[16,4,128,128]{3,2,1,0:T(8,128)(2,1)}, bf16[16,4,128,128]{3,2,1,0:T(8,128)(2,1)}, u32[]{:S(2)}, u32[]{:S(2)}) collective-permute-start(bf16[16,4,128,128]{3,2,1,0:T(8,128)(2,1)} %param.1), channel_id=1, source_target_pairs={{0,16},{16,0},{32,48},{48,32},{64,80},{80,64},{96,112},{112,96},{1... | collective-permute-start | bytes 6291464 | tf_op jit(solution)/shard_map/cond/branch_1_fun/ppermute | solution.py:189
